TPU v7x, 32 devices: a whole 2x2x4 slice. The times are simulated.
32 devices in a mesh: gx: 8 (over z, y), gy: 4 (over x, core).
Axes of the slice: x: 2, y: 2, z: 4, core: 2. Of those that a mesh axis runs over, the one named last changes fastest.
Arguments:
- state_in: float32 [5, 16, 32, 32, 128], P(None, None, 'gx', 'gy'), may hold values from -6 to 6
- sponge: float32 [32, 32, 128], P('gx', 'gy'), may hold values from 0.05 to 0.5
- mean_velocity: float32 [3], replicated, may hold values from -0.6 to 0.6
- wall_vector: float32 [5], replicated, may hold values from -3 to 3
- mode_shapes: float32 [16, 8192], P(None, ('gx', 'gy')), may hold values from -6 to 6
- wall_nodes: int32 [4, 32, 128], P(None, 'gx'), may hold values from 0 to 8191
- wall_weights: float32 [4, 32, 128], P(None, 'gx'), may hold values from 0.1 to 1
- wall_count: int32 [32], P('gx'), may hold values from 32 to 128
Outputs:
- state_out: float32 [5, 16, 32, 32, 128], P(None, None, 'gx', 'gy')
- r_factor: float32 [32, 32], replicated
All inputs are finite; a program needn't handle non-finite values.
Results may differ from a plain program's by a relative error of at most 0.00013.
Values sent between devices are 32-bit elements; how exact they have to be, the bound alone decides.
No kernel may reach another device: no remote copies, remote signals or barrier semaphores. Data moves between devices by JAX's collectives and lax.ppermute only.
A program may use at most 192 MiB of HBM per device.

v0:
```python
import math
import jax
import jax.numpy as jnp
import numpy as np
from jax import lax
from jax.sharding import PartitionSpec as P

STEPS = 2
C_SOUND = 1.0
NU_DAMP = 0.25
DT_STEP = 0.4
PULSE_MID = 0.8
PULSE_WIDTH = 0.5


def padded_2(x, sides, width):
    for axis, dim in sides:
        size, length = (lax.axis_size(axis), x.shape[dim])
        up = [(i, (i + 1) % size) for i in range(size - 1)]
        down = [(j, i) for i, j in up]
        last = lax.slice_in_dim(x, length - width, length, axis=dim)
        initial = lax.slice_in_dim(x, 0, width, axis=dim)
        before = lax.ppermute(last, axis, up)
        after = lax.ppermute(initial, axis, down)
        x = jnp.concatenate([before, x, after], axis=dim)
    return x


def pulse(time_now):
    return math.exp(-(((time_now - PULSE_MID) / PULSE_WIDTH) ** 2))


def jacobians(velocity):
    identity = jnp.eye(5, dtype=velocity.dtype)
    matrices = []
    for dimension in range(3):
        coupling = np.zeros((5, 5))
        coupling[0, 1 + dimension] = 1.0
        coupling[1 + dimension, 4] = 1.0
        coupling[4, 1 + dimension] = C_SOUND * C_SOUND
        matrices.append(velocity[dimension] * identity + jnp.asarray(coupling, velocity.dtype))
    return jnp.stack(matrices)


def rates(padded, jacobian, sponge_here, wall_rows, wall_line):
    highest = lax.Precision.HIGHEST
    center = padded[:, :, 1:-1, 1:-1, :]
    east_side = padded[:, :, 2:, 1:-1, :]
    west_side = padded[:, :, :-2, 1:-1, :]
    north_side = padded[:, :, 1:-1, 2:, :]
    south_side = padded[:, :, 1:-1, :-2, :]
    zero_plane = jnp.zeros_like(center[..., :1])
    upper_side = jnp.concatenate([center[..., 1:], zero_plane], axis=4)
    lower_side = jnp.concatenate([zero_plane, center[..., :-1]], axis=4)
    flux_sum = (
        jnp.einsum("fg,gmxyz->fmxyz", jacobian[0], east_side - west_side, precision=highest)
        + jnp.einsum("fg,gmxyz->fmxyz", jacobian[1], north_side - south_side, precision=highest)
        + jnp.einsum("fg,gmxyz->fmxyz", jacobian[2], upper_side - lower_side, precision=highest)
    )
    source = wall_rows[:, :, :, None, :] * wall_line[None, None, None, :, None]
    neighbours = east_side + west_side + north_side + south_side + upper_side + lower_side
    return (
        -0.5 * flux_sum
        + NU_DAMP * (neighbours - 6.0 * center)
        - sponge_here[None, None] * center
        + source
    )


def gather_terms(node_piece, local_pos, weights):
    piece_size = node_piece.shape[1]
    inside = (local_pos >= 0) & (local_pos < piece_size)
    values_taken = jnp.take(node_piece, jnp.clip(local_pos, 0, piece_size - 1), axis=1)
    return jnp.sum(jnp.where(inside, weights, 0.0)[None] * values_taken, axis=1)


def face_rate(field_state, jacobian, sponge, wall_rows, wall_line):
    padded = padded_2(field_state, (("gx", 2), ("gy", 3)), 1)
    return rates(padded, jacobian, sponge, wall_rows, wall_line)


def runge_step(state, rate_fn, time_now):
    rate_one = rate_fn(state, time_now)
    rate_two = rate_fn(state + 0.5 * DT_STEP * rate_one, time_now + 0.5 * DT_STEP)
    rate_three = rate_fn(state + 0.5 * DT_STEP * rate_two, time_now + 0.5 * DT_STEP)
    rate_four = rate_fn(state + DT_STEP * rate_three, time_now + DT_STEP)
    return state + DT_STEP / 6.0 * (rate_one + 2.0 * rate_two + 2.0 * rate_three + rate_four)


def local(
    state_in, sponge, mean_velocity, wall_vector, mode_shapes, wall_nodes, wall_weights, wall_count
):
    modes_here = state_in.shape[1]
    cells_x = state_in.shape[2]
    cells_y = state_in.shape[3]
    cells_z = state_in.shape[4]
    gx_size = lax.axis_size("gx")
    gy_size = lax.axis_size("gy")
    gy_here = lax.axis_index("gy")
    jacobian = jacobians(mean_velocity)
    forcing = gather_terms(
        lax.all_gather(mode_shapes, ("gx", "gy"), axis=1, tiled=True), wall_nodes, wall_weights
    )
    wall_mask = (jnp.arange(cells_z)[None, :] < wall_count[:, None]).astype(jnp.float32)
    forcing = forcing * wall_mask[None]
    wall_rows = wall_vector[:, None, None, None] * forcing[None]
    state = state_in
    wall_base = (jnp.arange(cells_y) + gy_here * cells_y == 0).astype(jnp.float32)

    def advance(state_now, time_now):

        def rate_fn(field_state, time_at):
            return face_rate(field_state, jacobian, sponge, wall_rows, wall_base * pulse(time_at))

        return runge_step(state_now, rate_fn, time_now)

    stacked = []
    for step in range(STEPS):
        state = advance(state, step * DT_STEP)
        stacked.append(state)
    rows_total = 5.0 * cells_x * gx_size * cells_y * gy_size * cells_z
    snap_count = STEPS * modes_here
    snapshots = jnp.stack(stacked)
    local_gram = jnp.einsum(
        "sfmxyz,tfnxyz->smtn", snapshots, snapshots, precision=lax.Precision.HIGHEST
    ).reshape(snap_count, snap_count)
    gram_matrix = lax.psum(local_gram, ("gx", "gy")) / rows_total
    r_factor = jnp.linalg.cholesky(gram_matrix).T
    return (stacked[-1], r_factor)


def solution(mesh):
    placed = (
        P(None, None, "gx", "gy", None),
        P("gx", "gy", None),
        P(),
        P(),
        P(None, ("gx", "gy")),
        P(None, "gx", None),
        P(None, "gx", None),
        P("gx"),
    )
    return jax.shard_map(
        local,
        mesh=mesh,
        in_specs=placed,
        out_specs=(P(None, None, "gx", "gy", None), P()),
        check_vma=False,
    )
```

profile of v0, /device:TPU:0, one launch (start us, length us, event | category | flops | bytes accessed | tf_op | source)
XLA Modules:
  0.0 501.3 jit_solution(947815659723375712)
XLA Ops:
  5.2 6.3 %collective-permute-start.1 = (f32[5,16,1,8,128]{4,0,3,2,1:T(8,128)}, f32[5,16,1,8,128]{4,0,3,2,1:T(8,128)}, u32[]{:S(2)}, u32[]{:S(2)}) collective-permute-start(f32[5,16,1,8,128]{4,0,3,2,1:T(8,128)} %get-tuple-element.53), channel_id=1, source_target_pairs={{0,4},{4,8},{8,12},{12,16},{16,20},{20,24},{24,28},{1,5},{5,9},{9,... | collective-permute-start | bytes 983048 | tf_op jit(solution)/shard_map/ppermute | solution.py:23
  15.2 62.8 %all_gather.3 = f32[16,8192]{0,1:T(8,128)} all-gather(f32[16,256]{0,1:T(8,128)S(1)} %copy.42), channel_id=1, replica_groups=mesh['gx'=8,'gy'=4] {'gx','gy'}, dimensions={1}, use_global_device_ids=true | all-gather | bytes 540672 | tf_op jit(solution)/shard_map/all_gather | solution.py:102
  78.1 7.7 %gather_fusion = f32[2048,16]{1,0:T(8,128)S(1)} fusion(f32[16,8192]{0,1:T(8,128)} %all_gather.3, s32[2048]{0:T(1024)S(1)} %broadcast_clamp_fusion), kind=kCustom, calls=%fused_computation | custom fusion | bytes 270336 | tf_op jit(solution)/shard_map/jit(_take)/gather | solution.py:73
  87.3 6.4 %fusion.63 = f32[5,16,4,8,128]{4,0,3,2,1:T(8,128)} fusion(f32[5,16,4,8,127]{4,0,3,2,1:T(8,128)} %get-tuple-element.55, f32[5,16,4,8,127]{4,0,3,2,1:T(8,128)} %get-tuple-element.54, f32[5,5]{1,0:T(8,128)S(1)} %copy-done.5, f32[]{:T(128)} %bitcast.6), kind=kOutput, calls=%fused_computation.127 | convolution fusion | flops 19988556 | bytes 3911784 | tf_op jit(solution)/shard_map/fg,gmxyz->fmxyz/dot_general | solution.py:58
  112.0 8.1 %multiply_add_fusion.13 = (f32[5,16,4,8,128]{4,0,3,2,1:T(8,128)S(1)}, f32[5,16,4,8,128]{4,0,3,2,1:T(8,128)S(1)}) fusion(f32[5,16,4,8,128]{4,3,2,1,0:T(8,128)S(1)} %copy-done.3, f32[8]{0:T(128)S(1)} %broadcast_select_fusion.3, f32[5,16,4,128]{3,0,2,1:T(8,128)S(1)} %broadcast_multiply_fusion, f32[4,8,128]{2,1,0:T(8,128)S(1)} %copy-done.7, ...), kind=kOutput, calls=%fused_computation.124 | convolution fusion | flops 27852876 | bytes 13758600 | tf_op jit(solution)/shard_map/fg,gmxyz->fmxyz/dot_general | solution.py:56
  131.3 8.5 %collective-permute-done.4 = f32[5,16,1,8,128]{4,0,3,2,1:T(8,128)S(1)} collective-permute-done((f32[5,16,1,8,128]{4,0,3,2,1:T(8,128)S(1)}, f32[5,16,1,8,128]{4,0,3,2,1:T(8,128)S(1)}, u32[]{:S(2)}, u32[]{:S(2)}) %collective-permute-start.4) | collective-permute-done | bytes 327712 | tf_op jit(solution)/shard_map/ppermute | solution.py:24
  139.9 9.8 %collective-permute-start.7 = (f32[5,16,6,1,128]{4,0,3,2,1:T(8,128)S(1)}, f32[5,16,6,1,128]{4,0,3,2,1:T(8,128)S(1)}, u32[]{:S(2)}, u32[]{:S(2)}) collective-permute-start(f32[5,16,6,1,128]{4,0,3,2,1:T(8,128)S(1)} %get-tuple-element.20), channel_id=1, source_target_pairs={{0,1},{1,2},{2,3},{4,5},{5,6},{6,7},{8,9},{9,10},{10,11},{12,13},{... | collective-permute-start | bytes 737288 | tf_op jit(solution)/shard_map/ppermute | solution.py:23
  156.3 7.6 %multiply_add_fusion.12 = (f32[5,16,4,8,128]{4,0,3,2,1:T(8,128)S(1)}, f32[5,16,4,8,128]{4,0,3,2,1:T(8,128)}) fusion(f32[5,16,4,8,128]{4,3,2,1,0:T(8,128)S(1)} %copy-done.3, f32[8]{0:T(128)S(1)} %broadcast_select_fusion.2, f32[5,16,4,128]{3,0,2,1:T(8,128)S(1)} %broadcast_multiply_fusion, f32[5,16,4,8,128]{4,0,3,2,1:T(8,128)S(1)} %get-tuple-element.59, ...), kind=kOutput, calls=%fused_computation.117 | convolution fusion | flops 29163596 | bytes 11792520 | tf_op jit(solution)/shard_map/fg,gmxyz->fmxyz/dot_general | solution.py:56
  175.8 9.8 %collective-permute-done.8 = f32[5,16,1,8,128]{4,0,3,2,1:T(8,128)S(1)} collective-permute-done((f32[5,16,1,8,128]{4,0,3,2,1:T(8,128)S(1)}, f32[5,16,1,8,128]{4,0,3,2,1:T(8,128)S(1)}, u32[]{:S(2)}, u32[]{:S(2)}) %collective-permute-start.8) | collective-permute-done | bytes 327712 | tf_op jit(solution)/shard_map/ppermute | solution.py:24
  185.7 8.0 %collective-permute-start.11 = (f32[5,16,6,1,128]{4,0,3,2,1:T(8,128)S(1)}, f32[5,16,6,1,128]{4,0,3,2,1:T(8,128)S(1)}, u32[]{:S(2)}, u32[]{:S(2)}) collective-permute-start(f32[5,16,6,1,128]{4,0,3,2,1:T(8,128)S(1)} %get-tuple-element.18), channel_id=1, source_target_pairs={{0,1},{1,2},{2,3},{4,5},{5,6},{6,7},{8,9},{9,10},{10,11},{12,13},{... | collective-permute-start | bytes 737288 | tf_op jit(solution)/shard_map/ppermute | solution.py:23
  200.6 7.5 %multiply_add_fusion.11 = (f32[5,16,4,8,128]{4,0,3,2,1:T(8,128)S(1)}, f32[5,16,4,8,128]{4,0,3,2,1:T(8,128)}) fusion(f32[5,16,4,8,128]{4,3,2,1,0:T(8,128)S(1)} %copy-done.3, f32[8]{0:T(128)S(1)} %broadcast_select_fusion.2, f32[5,16,4,128]{3,0,2,1:T(8,128)S(1)} %broadcast_multiply_fusion, f32[5,16,4,8,128]{4,0,3,2,1:T(8,128)S(1)} %get-tuple-element.61, ...), kind=kOutput, calls=%fused_computation.110 | convolution fusion | flops 29163596 | bytes 11792520 | tf_op jit(solution)/shard_map/fg,gmxyz->fmxyz/dot_general | solution.py:56
  219.8 11.1 %collective-permute-done.12 = f32[5,16,1,8,128]{4,0,3,2,1:T(8,128)S(1)} collective-permute-done((f32[5,16,1,8,128]{4,0,3,2,1:T(8,128)S(1)}, f32[5,16,1,8,128]{4,0,3,2,1:T(8,128)S(1)}, u32[]{:S(2)}, u32[]{:S(2)}) %collective-permute-start.12) | collective-permute-done | bytes 327712 | tf_op jit(solution)/shard_map/ppermute | solution.py:24
  244.4 8.5 %fusion.6 = f32[5,16,4,8,128]{4,0,3,2,1:T(8,128)S(1)} fusion(f32[5,16,4,8,128]{4,0,3,2,1:T(8,128)S(1)} %get-tuple-element.63, f32[5,16,4,8,128]{4,0,3,2,1:T(8,128)S(1)} %fusion.39, f32[5,16,4,8,128]{4,0,3,2,1:T(8,128)S(1)} %fusion.41, f32[5,16,1,8,128]{4,0,3,2,1:T(8,128)S(1)} %collective-permute-done.12, ...), kind=kOutput, calls=%fused_computation.14 | convolution fusion | flops 32112716 | bytes 14413992 | tf_op jit(solution)/shard_map/fg,gmxyz->fmxyz/dot_general | solution.py:56
  264.7 12.4 %collective-permute-done.16 = f32[5,16,1,8,128]{4,0,3,2,1:T(8,128)S(1)} collective-permute-done((f32[5,16,1,8,128]{4,0,3,2,1:T(8,128)S(1)}, f32[5,16,1,8,128]{4,0,3,2,1:T(8,128)S(1)}, u32[]{:S(2)}, u32[]{:S(2)}) %collective-permute-start.16) | collective-permute-done | bytes 327712 | tf_op jit(solution)/shard_map/ppermute | solution.py:24
  277.1 6.2 %collective-permute-start.19 = (f32[5,16,6,1,128]{4,0,3,2,1:T(8,128)S(1)}, f32[5,16,6,1,128]{4,0,3,2,1:T(8,128)S(1)}, u32[]{:S(2)}, u32[]{:S(2)}) collective-permute-start(f32[5,16,6,1,128]{4,0,3,2,1:T(8,128)S(1)} %get-tuple-element.14), channel_id=1, source_target_pairs={{0,1},{1,2},{2,3},{4,5},{5,6},{6,7},{8,9},{9,10},{10,11},{12,13},{... | collective-permute-start | bytes 737288 | tf_op jit(solution)/shard_map/ppermute | solution.py:23
  309.2 11.8 %collective-permute-done.20 = f32[5,16,1,8,128]{4,0,3,2,1:T(8,128)S(1)} collective-permute-done((f32[5,16,1,8,128]{4,0,3,2,1:T(8,128)S(1)}, f32[5,16,1,8,128]{4,0,3,2,1:T(8,128)S(1)}, u32[]{:S(2)}, u32[]{:S(2)}) %collective-permute-start.20) | collective-permute-done | bytes 327712 | tf_op jit(solution)/shard_map/ppermute | solution.py:24
  321.0 6.3 %collective-permute-start.23 = (f32[5,16,6,1,128]{4,0,3,2,1:T(8,128)S(1)}, f32[5,16,6,1,128]{4,0,3,2,1:T(8,128)S(1)}, u32[]{:S(2)}, u32[]{:S(2)}) collective-permute-start(f32[5,16,6,1,128]{4,0,3,2,1:T(8,128)S(1)} %get-tuple-element.12), channel_id=1, source_target_pairs={{0,1},{1,2},{2,3},{4,5},{5,6},{6,7},{8,9},{9,10},{10,11},{12,13},{... | collective-permute-start | bytes 737288 | tf_op jit(solution)/shard_map/ppermute | solution.py:23
  351.7 11.8 %collective-permute-done.24 = f32[5,16,1,8,128]{4,0,3,2,1:T(8,128)S(1)} collective-permute-done((f32[5,16,1,8,128]{4,0,3,2,1:T(8,128)S(1)}, f32[5,16,1,8,128]{4,0,3,2,1:T(8,128)S(1)}, u32[]{:S(2)}, u32[]{:S(2)}) %collective-permute-start.24) | collective-permute-done | bytes 327712 | tf_op jit(solution)/shard_map/ppermute | solution.py:24
  363.6 6.3 %collective-permute-start.27 = (f32[5,16,6,1,128]{4,0,3,2,1:T(8,128)S(1)}, f32[5,16,6,1,128]{4,0,3,2,1:T(8,128)S(1)}, u32[]{:S(2)}, u32[]{:S(2)}) collective-permute-start(f32[5,16,6,1,128]{4,0,3,2,1:T(8,128)S(1)} %get-tuple-element.10), channel_id=1, source_target_pairs={{0,1},{1,2},{2,3},{4,5},{5,6},{6,7},{8,9},{9,10},{10,11},{12,13},{... | collective-permute-start | bytes 737288 | tf_op jit(solution)/shard_map/ppermute | solution.py:23
  395.3 11.8 %collective-permute-done.28 = f32[5,16,1,8,128]{4,0,3,2,1:T(8,128)S(1)} collective-permute-done((f32[5,16,1,8,128]{4,0,3,2,1:T(8,128)S(1)}, f32[5,16,1,8,128]{4,0,3,2,1:T(8,128)S(1)}, u32[]{:S(2)}, u32[]{:S(2)}) %collective-permute-start.28) | collective-permute-done | bytes 327712 | tf_op jit(solution)/shard_map/ppermute | solution.py:24
  407.2 6.7 %collective-permute-start.31 = (f32[5,16,6,1,128]{4,0,3,2,1:T(8,128)S(1)}, f32[5,16,6,1,128]{4,0,3,2,1:T(8,128)S(1)}, u32[]{:S(2)}, u32[]{:S(2)}) collective-permute-start(f32[5,16,6,1,128]{4,0,3,2,1:T(8,128)S(1)} %get-tuple-element.8), channel_id=1, source_target_pairs={{0,1},{1,2},{2,3},{4,5},{5,6},{6,7},{8,9},{9,10},{10,11},{12,13},{... | collective-permute-start | bytes 737288 | tf_op jit(solution)/shard_map/ppermute | solution.py:23
  422.3 7.5 %multiply_add_fusion.6 = f32[5,16,4,8,128]{4,0,3,2,1:T(8,128)S(1)} fusion(f32[5,16,4,8,128]{4,0,3,2,1:T(8,128)S(1)} %fusion.6, f32[5,16,4,8,128]{4,0,3,2,1:T(8,128)S(1)} %get-tuple-element.69, f32[5,16,4,8,128]{4,0,3,2,1:T(8,128)S(1)} %fusion.7, f32[5,16,4,8,128]{4,0,3,2,1:T(8,128)} %fusion.9, f32[5,16,1,8,128]{4,0,3,2,1:T(8,128)S(1)} %collective-permute-done.28, ...), kind=kOutput, calls=%fused_computation.75 | convolution fusion | flops 32112716 | bytes 14413992 | tf_op jit(solution)/shard_map/fg,gmxyz->fmxyz/dot_general | solution.py:56
  432.2 11.1 %fusion.87 = f32[2,16,2,16]{3,1,2,0:T(8,128)S(1)} fusion(f32[2,5,16,4,8,128]{5,1,4,3,2,0:T(8,128)S(1)} %get-tuple-element.7, f32[2,5,16,4,8,128,1]{5,1,4,3,2,0,6:T(8,128)S(1)} %get-tuple-element.6), kind=kOutput, calls=%fused_computation.150 | convolution fusion | flops 251658240 | bytes 5246976 | tf_op jit(solution)/shard_map/sfmxyz,tfnxyz->smtn/dot_general | solution.py:124
  443.5 52.5 %psum.7 = f32[32,32]{0,1:T(8,128)S(1)} all-reduce(f32[32,32]{0,1:T(8,128)S(1)} %reshape.62), channel_id=1, replica_groups=mesh['gx'=8,'gy'=4] {'gx','gy'}, use_global_device_ids=true, to_apply=%region_1.2 | all-reduce | flops 1024 | bytes 8192 | tf_op jit(solution)/shard_map/psum | solution.py:127
  (154 shorter events, 193.1 us)
Async XLA Ops:
  3.9 91.8 %collective-permute-start = (f32[5,16,1,8,128]{4,0,3,2,1:T(8,128)}, f32[5,16,1,8,128]{4,0,3,2,1:T(8,128)}, u32[]{:S(2)}, u32[]{:S(2)}) collective-permute-start(f32[5,16,1,8,128]{4,0,3,2,1:T(8,128)} %get-tuple-element.52), channel_id=1, source_target_pairs={{4,0},{8,4},{12,8},{16,12},{20,16},{24,20},{28,24},{5,1},{9,5},{13... | collective-permute-start | bytes 983048 | tf_op jit(solution)/shard_map/ppermute | solution.py:24
  5.2 88.5 %collective-permute-start.1 = (f32[5,16,1,8,128]{4,0,3,2,1:T(8,128)}, f32[5,16,1,8,128]{4,0,3,2,1:T(8,128)}, u32[]{:S(2)}, u32[]{:S(2)}) collective-permute-start(f32[5,16,1,8,128]{4,0,3,2,1:T(8,128)} %get-tuple-element.53), channel_id=1, source_target_pairs={{0,4},{4,8},{8,12},{12,16},{16,20},{20,24},{24,28},{1,5},{5,9},{9,... | collective-permute-start | bytes 983048 | tf_op jit(solution)/shard_map/ppermute | solution.py:23
  99.5 5.5 %collective-permute-start.3 = (f32[5,16,6,1,128]{4,0,3,2,1:T(8,128)}, f32[5,16,6,1,128]{4,0,3,2,1:T(8,128)}, u32[]{:S(2)}, u32[]{:S(2)}) collective-permute-start(f32[5,16,6,1,128]{4,0,3,2,1:T(8,128)} %get-tuple-element.22), channel_id=1, source_target_pairs={{0,1},{1,2},{2,3},{4,5},{5,6},{6,7},{8,9},{9,10},{10,11},{12,13},{... | collective-permute-start | bytes 737288 | tf_op jit(solution)/shard_map/ppermute | solution.py:23
  120.2 11.0 %collective-permute-start.5 = (f32[5,16,1,8,128]{4,0,3,2,1:T(8,128)S(1)}, f32[5,16,1,8,128]{4,0,3,2,1:T(8,128)S(1)}, u32[]{:S(2)}, u32[]{:S(2)}) collective-permute-start(f32[5,16,1,8,128]{4,0,3,2,1:T(8,128)S(1)} %get-tuple-element.48), channel_id=1, source_target_pairs={{0,4},{4,8},{8,12},{12,16},{16,20},{20,24},{24,28},{1,5},{5,9},{9,... | collective-permute-start | bytes 983048 | tf_op jit(solution)/shard_map/ppermute | solution.py:23
  124.1 15.7 %collective-permute-start.4 = (f32[5,16,1,8,128]{4,0,3,2,1:T(8,128)S(1)}, f32[5,16,1,8,128]{4,0,3,2,1:T(8,128)S(1)}, u32[]{:S(2)}, u32[]{:S(2)}) collective-permute-start(f32[5,16,1,8,128]{4,0,3,2,1:T(8,128)S(1)} %get-tuple-element.49), channel_id=1, source_target_pairs={{4,0},{8,4},{12,8},{16,12},{20,16},{24,20},{28,24},{5,1},{9,5},{13... | collective-permute-start | bytes 983048 | tf_op jit(solution)/shard_map/ppermute | solution.py:24
  139.9 14.0 %collective-permute-start.7 = (f32[5,16,6,1,128]{4,0,3,2,1:T(8,128)S(1)}, f32[5,16,6,1,128]{4,0,3,2,1:T(8,128)S(1)}, u32[]{:S(2)}, u32[]{:S(2)}) collective-permute-start(f32[5,16,6,1,128]{4,0,3,2,1:T(8,128)S(1)} %get-tuple-element.20), channel_id=1, source_target_pairs={{0,1},{1,2},{2,3},{4,5},{5,6},{6,7},{8,9},{9,10},{10,11},{12,13},{... | collective-permute-start | bytes 737288 | tf_op jit(solution)/shard_map/ppermute | solution.py:23
  164.0 11.8 %collective-permute-start.9 = (f32[5,16,1,8,128]{4,0,3,2,1:T(8,128)S(1)}, f32[5,16,1,8,128]{4,0,3,2,1:T(8,128)S(1)}, u32[]{:S(2)}, u32[]{:S(2)}) collective-permute-start(f32[5,16,1,8,128]{4,0,3,2,1:T(8,128)S(1)} %get-tuple-element.44), channel_id=1, source_target_pairs={{0,4},{4,8},{8,12},{12,16},{16,20},{20,24},{24,28},{1,5},{5,9},{9,... | collective-permute-start | bytes 983048 | tf_op jit(solution)/shard_map/ppermute | solution.py:23
  168.1 17.5 %collective-permute-start.8 = (f32[5,16,1,8,128]{4,0,3,2,1:T(8,128)S(1)}, f32[5,16,1,8,128]{4,0,3,2,1:T(8,128)S(1)}, u32[]{:S(2)}, u32[]{:S(2)}) collective-permute-start(f32[5,16,1,8,128]{4,0,3,2,1:T(8,128)S(1)} %get-tuple-element.45), channel_id=1, source_target_pairs={{4,0},{8,4},{12,8},{16,12},{20,16},{24,20},{28,24},{5,1},{9,5},{13... | collective-permute-start | bytes 983048 | tf_op jit(solution)/shard_map/ppermute | solution.py:24
  185.7 12.4 %collective-permute-start.11 = (f32[5,16,6,1,128]{4,0,3,2,1:T(8,128)S(1)}, f32[5,16,6,1,128]{4,0,3,2,1:T(8,128)S(1)}, u32[]{:S(2)}, u32[]{:S(2)}) collective-permute-start(f32[5,16,6,1,128]{4,0,3,2,1:T(8,128)S(1)} %get-tuple-element.18), channel_id=1, source_target_pairs={{0,1},{1,2},{2,3},{4,5},{5,6},{6,7},{8,9},{9,10},{10,11},{12,13},{... | collective-permute-start | bytes 737288 | tf_op jit(solution)/shard_map/ppermute | solution.py:23
  208.1 11.7 %collective-permute-start.13 = (f32[5,16,1,8,128]{4,0,3,2,1:T(8,128)S(1)}, f32[5,16,1,8,128]{4,0,3,2,1:T(8,128)S(1)}, u32[]{:S(2)}, u32[]{:S(2)}) collective-permute-start(f32[5,16,1,8,128]{4,0,3,2,1:T(8,128)S(1)} %get-tuple-element.40), channel_id=1, source_target_pairs={{0,4},{4,8},{8,12},{12,16},{16,20},{20,24},{24,28},{1,5},{5,9},{9,... | collective-permute-start | bytes 983048 | tf_op jit(solution)/shard_map/ppermute | solution.py:23
  212.2 18.6 %collective-permute-start.12 = (f32[5,16,1,8,128]{4,0,3,2,1:T(8,128)S(1)}, f32[5,16,1,8,128]{4,0,3,2,1:T(8,128)S(1)}, u32[]{:S(2)}, u32[]{:S(2)}) collective-permute-start(f32[5,16,1,8,128]{4,0,3,2,1:T(8,128)S(1)} %get-tuple-element.41), channel_id=1, source_target_pairs={{4,0},{8,4},{12,8},{16,12},{20,16},{24,20},{28,24},{5,1},{9,5},{13... | collective-permute-start | bytes 983048 | tf_op jit(solution)/shard_map/ppermute | solution.py:24
  230.9 10.5 %collective-permute-start.15 = (f32[5,16,6,1,128]{4,0,3,2,1:T(8,128)S(1)}, f32[5,16,6,1,128]{4,0,3,2,1:T(8,128)S(1)}, u32[]{:S(2)}, u32[]{:S(2)}) collective-permute-start(f32[5,16,6,1,128]{4,0,3,2,1:T(8,128)S(1)} %get-tuple-element.16), channel_id=1, source_target_pairs={{0,1},{1,2},{2,3},{4,5},{5,6},{6,7},{8,9},{9,10},{10,11},{12,13},{... | collective-permute-start | bytes 737288 | tf_op jit(solution)/shard_map/ppermute | solution.py:23
  253.0 11.7 %collective-permute-start.17 = (f32[5,16,1,8,128]{4,0,3,2,1:T(8,128)S(1)}, f32[5,16,1,8,128]{4,0,3,2,1:T(8,128)S(1)}, u32[]{:S(2)}, u32[]{:S(2)}) collective-permute-start(f32[5,16,1,8,128]{4,0,3,2,1:T(8,128)S(1)} %get-tuple-element.36), channel_id=1, source_target_pairs={{0,4},{4,8},{8,12},{12,16},{16,20},{20,24},{24,28},{1,5},{5,9},{9,... | collective-permute-start | bytes 983048 | tf_op jit(solution)/shard_map/ppermute | solution.py:23
  257.4 19.6 %collective-permute-start.16 = (f32[5,16,1,8,128]{4,0,3,2,1:T(8,128)S(1)}, f32[5,16,1,8,128]{4,0,3,2,1:T(8,128)S(1)}, u32[]{:S(2)}, u32[]{:S(2)}) collective-permute-start(f32[5,16,1,8,128]{4,0,3,2,1:T(8,128)S(1)} %get-tuple-element.37), channel_id=1, source_target_pairs={{4,0},{8,4},{12,8},{16,12},{20,16},{24,20},{28,24},{5,1},{9,5},{13... | collective-permute-start | bytes 983048 | tf_op jit(solution)/shard_map/ppermute | solution.py:24
  277.1 10.7 %collective-permute-start.19 = (f32[5,16,6,1,128]{4,0,3,2,1:T(8,128)S(1)}, f32[5,16,6,1,128]{4,0,3,2,1:T(8,128)S(1)}, u32[]{:S(2)}, u32[]{:S(2)}) collective-permute-start(f32[5,16,6,1,128]{4,0,3,2,1:T(8,128)S(1)} %get-tuple-element.14), channel_id=1, source_target_pairs={{0,1},{1,2},{2,3},{4,5},{5,6},{6,7},{8,9},{9,10},{10,11},{12,13},{... | collective-permute-start | bytes 737288 | tf_op jit(solution)/shard_map/ppermute | solution.py:23
  296.5 12.7 %collective-permute-start.21 = (f32[5,16,1,8,128]{4,0,3,2,1:T(8,128)S(1)}, f32[5,16,1,8,128]{4,0,3,2,1:T(8,128)S(1)}, u32[]{:S(2)}, u32[]{:S(2)}) collective-permute-start(f32[5,16,1,8,128]{4,0,3,2,1:T(8,128)S(1)} %get-tuple-element.32), channel_id=1, source_target_pairs={{0,4},{4,8},{8,12},{12,16},{16,20},{20,24},{24,28},{1,5},{5,9},{9,... | collective-permute-start | bytes 983048 | tf_op jit(solution)/shard_map/ppermute | solution.py:23
  301.3 19.6 %collective-permute-start.20 = (f32[5,16,1,8,128]{4,0,3,2,1:T(8,128)S(1)}, f32[5,16,1,8,128]{4,0,3,2,1:T(8,128)S(1)}, u32[]{:S(2)}, u32[]{:S(2)}) collective-permute-start(f32[5,16,1,8,128]{4,0,3,2,1:T(8,128)S(1)} %get-tuple-element.33), channel_id=1, source_target_pairs={{4,0},{8,4},{12,8},{16,12},{20,16},{24,20},{28,24},{5,1},{9,5},{13... | collective-permute-start | bytes 983048 | tf_op jit(solution)/shard_map/ppermute | solution.py:24
  321.0 10.9 %collective-permute-start.23 = (f32[5,16,6,1,128]{4,0,3,2,1:T(8,128)S(1)}, f32[5,16,6,1,128]{4,0,3,2,1:T(8,128)S(1)}, u32[]{:S(2)}, u32[]{:S(2)}) collective-permute-start(f32[5,16,6,1,128]{4,0,3,2,1:T(8,128)S(1)} %get-tuple-element.12), channel_id=1, source_target_pairs={{0,1},{1,2},{2,3},{4,5},{5,6},{6,7},{8,9},{9,10},{10,11},{12,13},{... | collective-permute-start | bytes 737288 | tf_op jit(solution)/shard_map/ppermute | solution.py:23
  339.0 12.7 %collective-permute-start.25 = (f32[5,16,1,8,128]{4,0,3,2,1:T(8,128)S(1)}, f32[5,16,1,8,128]{4,0,3,2,1:T(8,128)S(1)}, u32[]{:S(2)}, u32[]{:S(2)}) collective-permute-start(f32[5,16,1,8,128]{4,0,3,2,1:T(8,128)S(1)} %get-tuple-element.28), channel_id=1, source_target_pairs={{0,4},{4,8},{8,12},{12,16},{16,20},{20,24},{24,28},{1,5},{5,9},{9,... | collective-permute-start | bytes 983048 | tf_op jit(solution)/shard_map/ppermute | solution.py:23
  343.9 19.6 %collective-permute-start.24 = (f32[5,16,1,8,128]{4,0,3,2,1:T(8,128)S(1)}, f32[5,16,1,8,128]{4,0,3,2,1:T(8,128)S(1)}, u32[]{:S(2)}, u32[]{:S(2)}) collective-permute-start(f32[5,16,1,8,128]{4,0,3,2,1:T(8,128)S(1)} %get-tuple-element.29), channel_id=1, source_target_pairs={{4,0},{8,4},{12,8},{16,12},{20,16},{24,20},{28,24},{5,1},{9,5},{13... | collective-permute-start | bytes 983048 | tf_op jit(solution)/shard_map/ppermute | solution.py:24
  363.6 10.7 %collective-permute-start.27 = (f32[5,16,6,1,128]{4,0,3,2,1:T(8,128)S(1)}, f32[5,16,6,1,128]{4,0,3,2,1:T(8,128)S(1)}, u32[]{:S(2)}, u32[]{:S(2)}) collective-permute-start(f32[5,16,6,1,128]{4,0,3,2,1:T(8,128)S(1)} %get-tuple-element.10), channel_id=1, source_target_pairs={{0,1},{1,2},{2,3},{4,5},{5,6},{6,7},{8,9},{9,10},{10,11},{12,13},{... | collective-permute-start | bytes 737288 | tf_op jit(solution)/shard_map/ppermute | solution.py:23
  383.1 12.3 %collective-permute-start.29 = (f32[5,16,1,8,128]{4,0,3,2,1:T(8,128)S(1)}, f32[5,16,1,8,128]{4,0,3,2,1:T(8,128)S(1)}, u32[]{:S(2)}, u32[]{:S(2)}) collective-permute-start(f32[5,16,1,8,128]{4,0,3,2,1:T(8,128)S(1)} %get-tuple-element.24), channel_id=1, source_target_pairs={{0,4},{4,8},{8,12},{12,16},{16,20},{20,24},{24,28},{1,5},{5,9},{9,... | collective-permute-start | bytes 983048 | tf_op jit(solution)/shard_map/ppermute | solution.py:23
  387.9 19.3 %collective-permute-start.28 = (f32[5,16,1,8,128]{4,0,3,2,1:T(8,128)S(1)}, f32[5,16,1,8,128]{4,0,3,2,1:T(8,128)S(1)}, u32[]{:S(2)}, u32[]{:S(2)}) collective-permute-start(f32[5,16,1,8,128]{4,0,3,2,1:T(8,128)S(1)} %get-tuple-element.25), channel_id=1, source_target_pairs={{4,0},{8,4},{12,8},{16,12},{20,16},{24,20},{28,24},{5,1},{9,5},{13... | collective-permute-start | bytes 983048 | tf_op jit(solution)/shard_map/ppermute | solution.py:24
  407.2 10.8 %collective-permute-start.31 = (f32[5,16,6,1,128]{4,0,3,2,1:T(8,128)S(1)}, f32[5,16,6,1,128]{4,0,3,2,1:T(8,128)S(1)}, u32[]{:S(2)}, u32[]{:S(2)}) collective-permute-start(f32[5,16,6,1,128]{4,0,3,2,1:T(8,128)S(1)} %get-tuple-element.8), channel_id=1, source_target_pairs={{0,1},{1,2},{2,3},{4,5},{5,6},{6,7},{8,9},{9,10},{10,11},{12,13},{... | collective-permute-start | bytes 737288 | tf_op jit(solution)/shard_map/ppermute | solution.py:23
  (23 other events, 126.8 us)
where the time goes:
time: 511 us; the launch traced here: 501 us
  matrix products  117 us (23%)
  waiting for transfers between devices  117 us (23%)
  blocking collectives  115 us (23%)
  starting transfers between devices  112 us (22%)
  local copies, waits for them, and re-layouts  29.7 us (6%)
  other arithmetic  7.58 us (1%)
    ppermute x16, starting transfers between devices, padded_2(): before = lax.ppermute(last, axis, up)  89.7 us
    ppermute x16, waiting for transfers between devices, padded_2(): after = lax.ppermute(initial, axis, down)  79.9 us
    all_gather x1, blocking collectives, local(): lax.all_gather(mode_shapes, ('gx', 'gy'), axis=1, tiled=True)  62.8 us
    dot_general x8, matrix products, rates(): jnp.einsum('fg,gmxyz->fmxyz', jacobian[0], east_side - west_side, precisi...  55.9 us
    psum x1, blocking collectives, local(): gram_matrix = lax.psum(local_gram, ('gx', 'gy')) / rows_total  52.5 us
    ppermute x16, waiting for transfers between devices, padded_2(): before = lax.ppermute(last, axis, up)  37.6 us
    dot_general x8, matrix products, rates(): jnp.einsum('fg,gmxyz->fmxyz', jacobian[2], upper_side - lower_side, preci...  26.5 us
    dot_general x8, matrix products, rates(): jnp.einsum('fg,gmxyz->fmxyz', jacobian[1], north_side - south_side, preci...  23.8 us
  transfers between devices with their start and end apart: 32, of which 17 were waited for; matrix products, arithmetic and copies ran while one was open for 10% of the time, Pallas kernels for 0%

commit v1 on v0

--- a/solution.py
+++ b/solution.py
@@ -11,6 +11,28 @@
 DT_STEP = 0.4
 PULSE_MID = 0.8
 PULSE_WIDTH = 0.5
+
+
+def in_order(blocks, dim):
+    blocks = jnp.moveaxis(blocks, 0, dim)
+    lengths = blocks.shape
+    return blocks.reshape(*lengths[:dim], lengths[dim] * lengths[dim + 1], *lengths[dim + 2 :])
+
+
+def doubled(x, axis):
+    length = lax.axis_size(axis)
+    tiles = x[None]
+    for level in range(length.bit_length() - 1):
+        bit = 1 << level
+        other = lax.ppermute(tiles, axis, [(i, i ^ bit) for i in range(length)])
+        both = jnp.stack([tiles, other])
+        upper = lax.axis_index(axis) >> level & 1
+        tiles = jnp.where(upper == 0, both, both[::-1]).reshape(-1, *x.shape)
+    return tiles
+
+
+def doubled_up(value, axis, dim):
+    return in_order(doubled(value, axis), dim)
 
 
 def padded_2(x, sides, width):
@@ -98,9 +120,7 @@
     gy_size = lax.axis_size("gy")
     gy_here = lax.axis_index("gy")
     jacobian = jacobians(mean_velocity)
-    forcing = gather_terms(
-        lax.all_gather(mode_shapes, ("gx", "gy"), axis=1, tiled=True), wall_nodes, wall_weights
-    )
+    forcing = gather_terms(doubled_up(mode_shapes, ("gx", "gy"), 1), wall_nodes, wall_weights)
     wall_mask = (jnp.arange(cells_z)[None, :] < wall_count[:, None]).astype(jnp.float32)
     forcing = forcing * wall_mask[None]
     wall_rows = wall_vector[:, None, None, None] * forcing[None]

time: 511 us -> 470 us (0.920)
  blocking collectives: 115 us -> 49.3 us
  starting transfers between devices: 112 us -> 132 us
  other arithmetic: 7.58 us -> 14.5 us
  local copies, waits for them, and re-layouts: 29.7 us -> 35.3 us
    all_gather x1 -> x0, blocking collectives: 62.8 us -> none  [local(): lax.all_gather(mode_shapes, ('gx', 'gy'), axis=1, tiled=True)]
    ppermute x16, waiting for transfers between devices: 79.9 us -> 28.4 us  [padded_2(): after = lax.ppermute(initial, axis, down)]
    ppermute x16, waiting for transfers between devices: 37.6 us -> 73.9 us  [padded_2(): before = lax.ppermute(last, axis, up)]
    ppermute x0 -> x5, waiting for transfers between devices: none -> 10.7 us  [doubled(): other = lax.ppermute(tiles, axis, [(i, i ^ bit) for i in range(length)])]
    ppermute x16, starting transfers between devices: 89.7 us -> 100 us  [padded_2(): before = lax.ppermute(last, axis, up)]
    ppermute x0 -> x5, starting transfers between devices: none -> 9.07 us  [doubled(): other = lax.ppermute(tiles, axis, [(i, i ^ bit) for i in range(length)])]
  transfers between devices with their start and end apart: 32 -> 37, of which waited for: 17 -> 19; matrix products, arithmetic and copies ran while one was open for 10% -> 14% of each run, Pallas kernels for 0% -> 0%
where the time goes in v1:
time: 470 us; the launch traced here: 463 us
  starting transfers between devices  132 us (28%)
  matrix products  117 us (25%)
  waiting for transfers between devices  113 us (24%)
  blocking collectives  49.3 us (10%)
  local copies, waits for them, and re-layouts  35.3 us (8%)
  other arithmetic  14.5 us (3%)
    ppermute x16, starting transfers between devices, padded_2(): before = lax.ppermute(last, axis, up)  100 us
    ppermute x16, waiting for transfers between devices, padded_2(): before = lax.ppermute(last, axis, up)  73.9 us
    dot_general x8, matrix products, rates(): jnp.einsum('fg,gmxyz->fmxyz', jacobian[0], east_side - west_side, precisi...  55.8 us
    psum x1, blocking collectives, local(): gram_matrix = lax.psum(local_gram, ('gx', 'gy')) / rows_total  49.3 us
    ppermute x16, waiting for transfers between devices, padded_2(): after = lax.ppermute(initial, axis, down)  28.4 us
    dot_general x8, matrix products, rates(): jnp.einsum('fg,gmxyz->fmxyz', jacobian[2], upper_side - lower_side, preci...  25.9 us
    dot_general x8, matrix products, rates(): jnp.einsum('fg,gmxyz->fmxyz', jacobian[1], north_side - south_side, preci...  24.5 us
    ppermute x16, starting transfers between devices, padded_2(): after = lax.ppermute(initial, axis, down)  22.7 us
  transfers between devices with their start and end apart: 37, of which 19 were waited for; matrix products, arithmetic and copies ran while one was open for 14% of the time, Pallas kernels for 0%

profile of v1, /device:TPU:0, one launch (start us, length us, event | category | flops | bytes accessed | tf_op | source)
XLA Modules:
  0.0 463.3 jit_solution(790995847828036709)
XLA Ops:
  5.7 5.9 %collective-permute-start.1 = (f32[5,16,1,8,128]{4,0,3,2,1:T(8,128)}, f32[5,16,1,8,128]{4,0,3,2,1:T(8,128)}, u32[]{:S(2)}, u32[]{:S(2)}) collective-permute-start(f32[5,16,1,8,128]{4,0,3,2,1:T(8,128)} %get-tuple-element.53), channel_id=1, source_target_pairs={{0,4},{4,8},{8,12},{12,16},{16,20},{20,24},{24,28},{1,5},{5,9},{9,... | collective-permute-start | bytes 983048 | tf_op jit(solution)/shard_map/ppermute | solution.py:45
  16.3 6.3 %fusion.63 = f32[5,16,4,8,128]{4,0,3,2,1:T(8,128)} fusion(f32[5,16,4,8,127]{4,0,3,2,1:T(8,128)} %get-tuple-element.55, f32[5,16,4,8,127]{4,0,3,2,1:T(8,128)} %get-tuple-element.54, f32[5,5]{1,0:T(8,128)S(1)} %copy-done.5, f32[]{:T(128)} %bitcast.6), kind=kOutput, calls=%fused_computation.127 | convolution fusion | flops 19988556 | bytes 3911784 | tf_op jit(solution)/shard_map/fg,gmxyz->fmxyz/dot_general | solution.py:80
  59.5 9.8 %gather_fusion = f32[2048,16]{1,0:T(8,128)} fusion(f32[16,8192]{0,1:T(8,128)} %bitcast.120, s32[2048]{0:T(1024)S(1)} %copy-done.7), kind=kCustom, calls=%fused_computation | custom fusion | bytes 270336 | tf_op jit(solution)/shard_map/jit(_take)/gather | solution.py:95
  78.7 8.2 %multiply_add_fusion.13 = (f32[5,16,4,8,128]{4,0,3,2,1:T(8,128)S(1)}, f32[5,16,4,8,128]{4,0,3,2,1:T(8,128)S(1)}) fusion(f32[5,16,4,8,128]{4,3,2,1,0:T(8,128)S(1)} %copy-done.3, f32[8]{0:T(128)S(1)} %copy-done.15, f32[5,16,4,128]{3,0,2,1:T(8,128)S(1)} %broadcast_multiply_fusion, f32[4,8,128]{2,1,0:T(8,128)S(1)} %copy-done.8, ...), kind=kOutput, calls=%fused_computation.124 | convolution fusion | flops 27852876 | bytes 13758600 | tf_op jit(solution)/shard_map/fg,gmxyz->fmxyz/dot_general | solution.py:78
  93.5 20.5 %collective-permute-done.10 = f32[5,16,1,8,128]{4,0,3,2,1:T(8,128)S(1)} collective-permute-done((f32[5,16,1,8,128]{4,0,3,2,1:T(8,128)S(1)}, f32[5,16,1,8,128]{4,0,3,2,1:T(8,128)S(1)}, u32[]{:S(2)}, u32[]{:S(2)}) %collective-permute-start.10) | collective-permute-done | bytes 327712 | tf_op jit(solution)/shard_map/ppermute | solution.py:45
  122.9 7.5 %multiply_add_fusion.12 = (f32[5,16,4,8,128]{4,0,3,2,1:T(8,128)S(1)}, f32[5,16,4,8,128]{4,0,3,2,1:T(8,128)}) fusion(f32[5,16,4,8,128]{4,3,2,1,0:T(8,128)S(1)} %copy-done.3, f32[8]{0:T(128)S(1)} %copy-done.21, f32[5,16,4,128]{3,0,2,1:T(8,128)S(1)} %broadcast_multiply_fusion, f32[5,16,4,8,128]{4,0,3,2,1:T(8,128)S(1)} %get-tuple-element.61, ...), kind=kOutput, calls=%fused_computation.117 | convolution fusion | flops 29163596 | bytes 11792520 | tf_op jit(solution)/shard_map/fg,gmxyz->fmxyz/dot_general | solution.py:78
  137.1 16.9 %collective-permute-done.14 = f32[5,16,1,8,128]{4,0,3,2,1:T(8,128)S(1)} collective-permute-done((f32[5,16,1,8,128]{4,0,3,2,1:T(8,128)S(1)}, f32[5,16,1,8,128]{4,0,3,2,1:T(8,128)S(1)}, u32[]{:S(2)}, u32[]{:S(2)}) %collective-permute-start.14) | collective-permute-done | bytes 327712 | tf_op jit(solution)/shard_map/ppermute | solution.py:45
  154.0 6.5 %collective-permute-start.16 = (f32[5,16,6,1,128]{4,0,3,2,1:T(8,128)S(1)}, f32[5,16,6,1,128]{4,0,3,2,1:T(8,128)S(1)}, u32[]{:S(2)}, u32[]{:S(2)}) collective-permute-start(f32[5,16,6,1,128]{4,0,3,2,1:T(8,128)S(1)} %get-tuple-element.18), channel_id=1, source_target_pairs={{0,1},{1,2},{2,3},{4,5},{5,6},{6,7},{8,9},{9,10},{10,11},{12,13},{... | collective-permute-start | bytes 737288 | tf_op jit(solution)/shard_map/ppermute | solution.py:45
  167.8 7.4 %multiply_add_fusion.11 = (f32[5,16,4,8,128]{4,0,3,2,1:T(8,128)S(1)}, f32[5,16,4,8,128]{4,0,3,2,1:T(8,128)}) fusion(f32[5,16,4,8,128]{4,3,2,1,0:T(8,128)S(1)} %copy-done.3, f32[8]{0:T(128)S(1)} %copy-done.21, f32[5,16,4,128]{3,0,2,1:T(8,128)S(1)} %broadcast_multiply_fusion, f32[5,16,4,8,128]{4,0,3,2,1:T(8,128)S(1)} %get-tuple-element.63, ...), kind=kOutput, calls=%fused_computation.110 | convolution fusion | flops 29163596 | bytes 11792520 | tf_op jit(solution)/shard_map/fg,gmxyz->fmxyz/dot_general | solution.py:78
  181.9 16.3 %collective-permute-done.18 = f32[5,16,1,8,128]{4,0,3,2,1:T(8,128)S(1)} collective-permute-done((f32[5,16,1,8,128]{4,0,3,2,1:T(8,128)S(1)}, f32[5,16,1,8,128]{4,0,3,2,1:T(8,128)S(1)}, u32[]{:S(2)}, u32[]{:S(2)}) %collective-permute-start.18) | collective-permute-done | bytes 327712 | tf_op jit(solution)/shard_map/ppermute | solution.py:45
  198.3 7.1 %collective-permute-start.20 = (f32[5,16,6,1,128]{4,0,3,2,1:T(8,128)S(1)}, f32[5,16,6,1,128]{4,0,3,2,1:T(8,128)S(1)}, u32[]{:S(2)}, u32[]{:S(2)}) collective-permute-start(f32[5,16,6,1,128]{4,0,3,2,1:T(8,128)S(1)} %get-tuple-element.16), channel_id=1, source_target_pairs={{0,1},{1,2},{2,3},{4,5},{5,6},{6,7},{8,9},{9,10},{10,11},{12,13},{... | collective-permute-start | bytes 737288 | tf_op jit(solution)/shard_map/ppermute | solution.py:45
  212.3 8.5 %fusion.6 = f32[5,16,4,8,128]{4,0,3,2,1:T(8,128)S(1)} fusion(f32[5,16,4,8,128]{4,0,3,2,1:T(8,128)S(1)} %get-tuple-element.65, f32[5,16,4,8,128]{4,0,3,2,1:T(8,128)S(1)} %fusion.39, f32[5,16,4,8,128]{4,0,3,2,1:T(8,128)S(1)} %fusion.41, f32[5,16,1,8,128]{4,0,3,2,1:T(8,128)S(1)} %collective-permute-done.17, ...), kind=kOutput, calls=%fused_computation.14 | convolution fusion | flops 32112716 | bytes 14413992 | tf_op jit(solution)/shard_map/fg,gmxyz->fmxyz/dot_general | solution.py:78
  238.0 13.0 %collective-permute-start.24 = (f32[5,16,6,1,128]{4,0,3,2,1:T(8,128)S(1)}, f32[5,16,6,1,128]{4,0,3,2,1:T(8,128)S(1)}, u32[]{:S(2)}, u32[]{:S(2)}) collective-permute-start(f32[5,16,6,1,128]{4,0,3,2,1:T(8,128)S(1)} %get-tuple-element.14), channel_id=1, source_target_pairs={{0,1},{1,2},{2,3},{4,5},{5,6},{6,7},{8,9},{9,10},{10,11},{12,13},{... | collective-permute-start | bytes 737288 | tf_op jit(solution)/shard_map/ppermute | solution.py:45
  257.9 6.0 %multiply_add_fusion.9 = (f32[5,16,4,8,128]{4,0,3,2,1:T(8,128)S(1)}, f32[5,16,4,8,128]{4,0,3,2,1:T(8,128)}) fusion(f32[5,16,4,8,128]{4,0,3,2,1:T(8,128)S(1)} %fusion.6, f32[8]{0:T(128)S(1)} %copy-done.18, f32[5,16,4,128]{3,0,2,1:T(8,128)S(1)} %broadcast_multiply_fusion, f32[4,8,128]{2,1,0:T(8,128)S(1)} %copy-done.8, ...), kind=kOutput, calls=%fused_computation.96 | convolution fusion | flops 29163596 | bytes 10481800 | tf_op jit(solution)/shard_map/fg,gmxyz->fmxyz/dot_general | solution.py:78
  275.6 6.3 %collective-permute-done.25 = f32[5,16,1,8,128]{4,0,3,2,1:T(8,128)S(1)} collective-permute-done((f32[5,16,1,8,128]{4,0,3,2,1:T(8,128)S(1)}, f32[5,16,1,8,128]{4,0,3,2,1:T(8,128)S(1)}, u32[]{:S(2)}, u32[]{:S(2)}) %collective-permute-start.25) | collective-permute-done | bytes 327712 | tf_op jit(solution)/shard_map/ppermute | solution.py:46
  282.0 12.1 %collective-permute-start.28 = (f32[5,16,6,1,128]{4,0,3,2,1:T(8,128)S(1)}, f32[5,16,6,1,128]{4,0,3,2,1:T(8,128)S(1)}, u32[]{:S(2)}, u32[]{:S(2)}) collective-permute-start(f32[5,16,6,1,128]{4,0,3,2,1:T(8,128)S(1)} %get-tuple-element.12), channel_id=1, source_target_pairs={{0,1},{1,2},{2,3},{4,5},{5,6},{6,7},{8,9},{9,10},{10,11},{12,13},{... | collective-permute-start | bytes 737288 | tf_op jit(solution)/shard_map/ppermute | solution.py:45
  317.3 7.2 %collective-permute-done.29 = f32[5,16,1,8,128]{4,0,3,2,1:T(8,128)S(1)} collective-permute-done((f32[5,16,1,8,128]{4,0,3,2,1:T(8,128)S(1)}, f32[5,16,1,8,128]{4,0,3,2,1:T(8,128)S(1)}, u32[]{:S(2)}, u32[]{:S(2)}) %collective-permute-start.29) | collective-permute-done | bytes 327712 | tf_op jit(solution)/shard_map/ppermute | solution.py:46
  324.6 11.2 %collective-permute-start.32 = (f32[5,16,6,1,128]{4,0,3,2,1:T(8,128)S(1)}, f32[5,16,6,1,128]{4,0,3,2,1:T(8,128)S(1)}, u32[]{:S(2)}, u32[]{:S(2)}) collective-permute-start(f32[5,16,6,1,128]{4,0,3,2,1:T(8,128)S(1)} %get-tuple-element.10), channel_id=1, source_target_pairs={{0,1},{1,2},{2,3},{4,5},{5,6},{6,7},{8,9},{9,10},{10,11},{12,13},{... | collective-permute-start | bytes 737288 | tf_op jit(solution)/shard_map/ppermute | solution.py:45
  343.0 6.1 %multiply_add_fusion.7 = (f32[5,16,4,8,128]{4,0,3,2,1:T(8,128)S(1)}, f32[5,16,4,8,128]{4,0,3,2,1:T(8,128)}) fusion(f32[5,16,4,8,128]{4,0,3,2,1:T(8,128)S(1)} %fusion.6, f32[8]{0:T(128)S(1)} %copy-done.20, f32[5,16,4,128]{3,0,2,1:T(8,128)S(1)} %broadcast_multiply_fusion, f32[5,16,4,8,128]{4,0,3,2,1:T(8,128)S(1)} %get-tuple-element.69, ...), kind=kOutput, calls=%fused_computation.82 | convolution fusion | flops 29163596 | bytes 11792520 | tf_op jit(solution)/shard_map/fg,gmxyz->fmxyz/dot_general | solution.py:78
  360.8 8.1 %collective-permute-done.33 = f32[5,16,1,8,128]{4,0,3,2,1:T(8,128)S(1)} collective-permute-done((f32[5,16,1,8,128]{4,0,3,2,1:T(8,128)S(1)}, f32[5,16,1,8,128]{4,0,3,2,1:T(8,128)S(1)}, u32[]{:S(2)}, u32[]{:S(2)}) %collective-permute-start.33) | collective-permute-done | bytes 327712 | tf_op jit(solution)/shard_map/ppermute | solution.py:46
  369.0 10.3 %collective-permute-start.36 = (f32[5,16,6,1,128]{4,0,3,2,1:T(8,128)S(1)}, f32[5,16,6,1,128]{4,0,3,2,1:T(8,128)S(1)}, u32[]{:S(2)}, u32[]{:S(2)}) collective-permute-start(f32[5,16,6,1,128]{4,0,3,2,1:T(8,128)S(1)} %get-tuple-element.8), channel_id=1, source_target_pairs={{0,1},{1,2},{2,3},{4,5},{5,6},{6,7},{8,9},{9,10},{10,11},{12,13},{... | collective-permute-start | bytes 737288 | tf_op jit(solution)/shard_map/ppermute | solution.py:45
  387.5 7.5 %multiply_add_fusion.6 = f32[5,16,4,8,128]{4,0,3,2,1:T(8,128)S(1)} fusion(f32[5,16,4,8,128]{4,0,3,2,1:T(8,128)S(1)} %fusion.6, f32[5,16,4,8,128]{4,0,3,2,1:T(8,128)S(1)} %get-tuple-element.71, f32[5,16,4,8,128]{4,0,3,2,1:T(8,128)S(1)} %fusion.7, f32[5,16,4,8,128]{4,0,3,2,1:T(8,128)} %fusion.9, f32[5,16,1,8,128]{4,0,3,2,1:T(8,128)S(1)} %collective-permute-done.33, ...), kind=kOutput, calls=%fused_computation.75 | convolution fusion | flops 32112716 | bytes 14413992 | tf_op jit(solution)/shard_map/fg,gmxyz->fmxyz/dot_general | solution.py:78
  397.4 11.1 %fusion.87 = f32[2,16,2,16]{3,1,2,0:T(8,128)S(1)} fusion(f32[2,5,16,4,8,128]{5,1,4,3,2,0:T(8,128)S(1)} %get-tuple-element.7, f32[2,5,16,4,8,128,1]{5,1,4,3,2,0,6:T(8,128)S(1)} %get-tuple-element.6), kind=kOutput, calls=%fused_computation.150 | convolution fusion | flops 251658240 | bytes 5246976 | tf_op jit(solution)/shard_map/sfmxyz,tfnxyz->smtn/dot_general | solution.py:144
  408.7 49.3 %psum.7 = f32[32,32]{0,1:T(8,128)S(1)} all-reduce(f32[32,32]{0,1:T(8,128)S(1)} %reshape.86), channel_id=1, replica_groups=mesh['gx'=8,'gy'=4] {'gx','gy'}, use_global_device_ids=true, to_apply=%region_1.2 | all-reduce | flops 1024 | bytes 8192 | tf_op jit(solution)/shard_map/psum | solution.py:147
  (187 shorter events, 192.3 us)
Async XLA Ops:
  0.6 22.5 %collective-permute-start.4 = (f32[1,16,256]{2,1,0:T(8,128)}, f32[1,16,256]{2,1,0:T(8,128)S(1)}, u32[]{:S(2)}, u32[]{:S(2)}) collective-permute-start(f32[1,16,256]{2,1,0:T(8,128)} %bitcast.133), channel_id=1, source_target_pairs={{0,1},{1,0},{2,3},{3,2},{4,5},{5,4},{6,7},{7,6},{8,9},{9,8},{10,11... | collective-permute-start | bytes 49160 | tf_op jit(solution)/shard_map/ppermute | solution.py:27
  4.4 41.3 %collective-permute-start = (f32[5,16,1,8,128]{4,0,3,2,1:T(8,128)}, f32[5,16,1,8,128]{4,0,3,2,1:T(8,128)}, u32[]{:S(2)}, u32[]{:S(2)}) collective-permute-start(f32[5,16,1,8,128]{4,0,3,2,1:T(8,128)} %get-tuple-element.52), channel_id=1, source_target_pairs={{4,0},{8,4},{12,8},{16,12},{20,16},{24,20},{28,24},{5,1},{9,5},{13... | collective-permute-start | bytes 983048 | tf_op jit(solution)/shard_map/ppermute | solution.py:46
  5.7 38.0 %collective-permute-start.1 = (f32[5,16,1,8,128]{4,0,3,2,1:T(8,128)}, f32[5,16,1,8,128]{4,0,3,2,1:T(8,128)}, u32[]{:S(2)}, u32[]{:S(2)}) collective-permute-start(f32[5,16,1,8,128]{4,0,3,2,1:T(8,128)} %get-tuple-element.53), channel_id=1, source_target_pairs={{0,4},{4,8},{8,12},{12,16},{16,20},{20,24},{24,28},{1,5},{5,9},{9,... | collective-permute-start | bytes 983048 | tf_op jit(solution)/shard_map/ppermute | solution.py:45
  41.1 14.0 %collective-permute-start.8 = (f32[16,16,256]{2,1,0:T(8,128)S(1)}, f32[16,16,256]{2,1,0:T(8,128)S(1)}, u32[]{:S(2)}, u32[]{:S(2)}) collective-permute-start(f32[16,16,256]{2,1,0:T(8,128)S(1)} %bitcast.123), channel_id=1, source_target_pairs={{0,16},{1,17},{2,18},{3,19},{4,20},{5,21},{6,22},{7,23},{8,24},{9,... | collective-permute-start | bytes 786440 | tf_op jit(solution)/shard_map/ppermute | solution.py:27
  49.4 23.7 %collective-permute-start.3 = (f32[5,16,6,1,128]{4,0,3,2,1:T(8,128)}, f32[5,16,6,1,128]{4,0,3,2,1:T(8,128)}, u32[]{:S(2)}, u32[]{:S(2)}) collective-permute-start(f32[5,16,6,1,128]{4,0,3,2,1:T(8,128)} %get-tuple-element.22), channel_id=1, source_target_pairs={{0,1},{1,2},{2,3},{4,5},{5,6},{6,7},{8,9},{9,10},{10,11},{12,13},{... | collective-permute-start | bytes 737288 | tf_op jit(solution)/shard_map/ppermute | solution.py:45
  51.4 21.7 %collective-permute-start.2 = (f32[5,16,6,1,128]{4,0,3,2,1:T(8,128)}, f32[5,16,6,1,128]{4,0,3,2,1:T(8,128)}, u32[]{:S(2)}, u32[]{:S(2)}) collective-permute-start(f32[5,16,6,1,128]{4,0,3,2,1:T(8,128)} %get-tuple-element.23), channel_id=1, source_target_pairs={{1,0},{2,1},{3,2},{5,4},{6,5},{7,6},{9,8},{10,9},{11,10},{13,12},{... | collective-permute-start | bytes 737288 | tf_op jit(solution)/shard_map/ppermute | solution.py:46
  86.9 27.1 %collective-permute-start.10 = (f32[5,16,1,8,128]{4,0,3,2,1:T(8,128)S(1)}, f32[5,16,1,8,128]{4,0,3,2,1:T(8,128)S(1)}, u32[]{:S(2)}, u32[]{:S(2)}) collective-permute-start(f32[5,16,1,8,128]{4,0,3,2,1:T(8,128)S(1)} %get-tuple-element.48), channel_id=1, source_target_pairs={{0,4},{4,8},{8,12},{12,16},{16,20},{20,24},{24,28},{1,5},{5,9},{9,... | collective-permute-start | bytes 983048 | tf_op jit(solution)/shard_map/ppermute | solution.py:45
  91.4 22.6 %collective-permute-start.9 = (f32[5,16,1,8,128]{4,0,3,2,1:T(8,128)S(1)}, f32[5,16,1,8,128]{4,0,3,2,1:T(8,128)S(1)}, u32[]{:S(2)}, u32[]{:S(2)}) collective-permute-start(f32[5,16,1,8,128]{4,0,3,2,1:T(8,128)S(1)} %get-tuple-element.49), channel_id=1, source_target_pairs={{4,0},{8,4},{12,8},{16,12},{20,16},{24,20},{28,24},{5,1},{9,5},{13... | collective-permute-start | bytes 983048 | tf_op jit(solution)/shard_map/ppermute | solution.py:46
  130.5 23.4 %collective-permute-start.14 = (f32[5,16,1,8,128]{4,0,3,2,1:T(8,128)S(1)}, f32[5,16,1,8,128]{4,0,3,2,1:T(8,128)S(1)}, u32[]{:S(2)}, u32[]{:S(2)}) collective-permute-start(f32[5,16,1,8,128]{4,0,3,2,1:T(8,128)S(1)} %get-tuple-element.44), channel_id=1, source_target_pairs={{0,4},{4,8},{8,12},{12,16},{16,20},{20,24},{24,28},{1,5},{5,9},{9,... | collective-permute-start | bytes 983048 | tf_op jit(solution)/shard_map/ppermute | solution.py:45
  134.9 19.0 %collective-permute-start.13 = (f32[5,16,1,8,128]{4,0,3,2,1:T(8,128)S(1)}, f32[5,16,1,8,128]{4,0,3,2,1:T(8,128)S(1)}, u32[]{:S(2)}, u32[]{:S(2)}) collective-permute-start(f32[5,16,1,8,128]{4,0,3,2,1:T(8,128)S(1)} %get-tuple-element.45), channel_id=1, source_target_pairs={{4,0},{8,4},{12,8},{16,12},{20,16},{24,20},{28,24},{5,1},{9,5},{13... | collective-permute-start | bytes 983048 | tf_op jit(solution)/shard_map/ppermute | solution.py:46
  175.3 22.9 %collective-permute-start.18 = (f32[5,16,1,8,128]{4,0,3,2,1:T(8,128)S(1)}, f32[5,16,1,8,128]{4,0,3,2,1:T(8,128)S(1)}, u32[]{:S(2)}, u32[]{:S(2)}) collective-permute-start(f32[5,16,1,8,128]{4,0,3,2,1:T(8,128)S(1)} %get-tuple-element.40), channel_id=1, source_target_pairs={{0,4},{4,8},{8,12},{12,16},{16,20},{20,24},{24,28},{1,5},{5,9},{9,... | collective-permute-start | bytes 983048 | tf_op jit(solution)/shard_map/ppermute | solution.py:45
  179.7 18.4 %collective-permute-start.17 = (f32[5,16,1,8,128]{4,0,3,2,1:T(8,128)S(1)}, f32[5,16,1,8,128]{4,0,3,2,1:T(8,128)S(1)}, u32[]{:S(2)}, u32[]{:S(2)}) collective-permute-start(f32[5,16,1,8,128]{4,0,3,2,1:T(8,128)S(1)} %get-tuple-element.41), channel_id=1, source_target_pairs={{4,0},{8,4},{12,8},{16,12},{20,16},{24,20},{28,24},{5,1},{9,5},{13... | collective-permute-start | bytes 983048 | tf_op jit(solution)/shard_map/ppermute | solution.py:46
  220.9 11.5 %collective-permute-start.22 = (f32[5,16,1,8,128]{4,0,3,2,1:T(8,128)S(1)}, f32[5,16,1,8,128]{4,0,3,2,1:T(8,128)S(1)}, u32[]{:S(2)}, u32[]{:S(2)}) collective-permute-start(f32[5,16,1,8,128]{4,0,3,2,1:T(8,128)S(1)} %get-tuple-element.36), channel_id=1, source_target_pairs={{0,4},{4,8},{8,12},{12,16},{16,20},{20,24},{24,28},{1,5},{5,9},{9,... | collective-permute-start | bytes 983048 | tf_op jit(solution)/shard_map/ppermute | solution.py:45
  225.3 12.6 %collective-permute-start.21 = (f32[5,16,1,8,128]{4,0,3,2,1:T(8,128)S(1)}, f32[5,16,1,8,128]{4,0,3,2,1:T(8,128)S(1)}, u32[]{:S(2)}, u32[]{:S(2)}) collective-permute-start(f32[5,16,1,8,128]{4,0,3,2,1:T(8,128)S(1)} %get-tuple-element.37), channel_id=1, source_target_pairs={{4,0},{8,4},{12,8},{16,12},{20,16},{24,20},{28,24},{5,1},{9,5},{13... | collective-permute-start | bytes 983048 | tf_op jit(solution)/shard_map/ppermute | solution.py:46
  238.0 17.4 %collective-permute-start.24 = (f32[5,16,6,1,128]{4,0,3,2,1:T(8,128)S(1)}, f32[5,16,6,1,128]{4,0,3,2,1:T(8,128)S(1)}, u32[]{:S(2)}, u32[]{:S(2)}) collective-permute-start(f32[5,16,6,1,128]{4,0,3,2,1:T(8,128)S(1)} %get-tuple-element.14), channel_id=1, source_target_pairs={{0,1},{1,2},{2,3},{4,5},{5,6},{6,7},{8,9},{9,10},{10,11},{12,13},{... | collective-permute-start | bytes 737288 | tf_op jit(solution)/shard_map/ppermute | solution.py:45
  264.1 11.6 %collective-permute-start.26 = (f32[5,16,1,8,128]{4,0,3,2,1:T(8,128)S(1)}, f32[5,16,1,8,128]{4,0,3,2,1:T(8,128)S(1)}, u32[]{:S(2)}, u32[]{:S(2)}) collective-permute-start(f32[5,16,1,8,128]{4,0,3,2,1:T(8,128)S(1)} %get-tuple-element.32), channel_id=1, source_target_pairs={{0,4},{4,8},{8,12},{12,16},{16,20},{20,24},{24,28},{1,5},{5,9},{9,... | collective-permute-start | bytes 983048 | tf_op jit(solution)/shard_map/ppermute | solution.py:45
  268.4 13.5 %collective-permute-start.25 = (f32[5,16,1,8,128]{4,0,3,2,1:T(8,128)S(1)}, f32[5,16,1,8,128]{4,0,3,2,1:T(8,128)S(1)}, u32[]{:S(2)}, u32[]{:S(2)}) collective-permute-start(f32[5,16,1,8,128]{4,0,3,2,1:T(8,128)S(1)} %get-tuple-element.33), channel_id=1, source_target_pairs={{4,0},{8,4},{12,8},{16,12},{20,16},{24,20},{28,24},{5,1},{9,5},{13... | collective-permute-start | bytes 983048 | tf_op jit(solution)/shard_map/ppermute | solution.py:46
  282.0 16.7 %collective-permute-start.28 = (f32[5,16,6,1,128]{4,0,3,2,1:T(8,128)S(1)}, f32[5,16,6,1,128]{4,0,3,2,1:T(8,128)S(1)}, u32[]{:S(2)}, u32[]{:S(2)}) collective-permute-start(f32[5,16,6,1,128]{4,0,3,2,1:T(8,128)S(1)} %get-tuple-element.12), channel_id=1, source_target_pairs={{0,1},{1,2},{2,3},{4,5},{5,6},{6,7},{8,9},{9,10},{10,11},{12,13},{... | collective-permute-start | bytes 737288 | tf_op jit(solution)/shard_map/ppermute | solution.py:45
  305.8 11.5 %collective-permute-start.30 = (f32[5,16,1,8,128]{4,0,3,2,1:T(8,128)S(1)}, f32[5,16,1,8,128]{4,0,3,2,1:T(8,128)S(1)}, u32[]{:S(2)}, u32[]{:S(2)}) collective-permute-start(f32[5,16,1,8,128]{4,0,3,2,1:T(8,128)S(1)} %get-tuple-element.28), channel_id=1, source_target_pairs={{0,4},{4,8},{8,12},{12,16},{16,20},{20,24},{24,28},{1,5},{5,9},{9,... | collective-permute-start | bytes 983048 | tf_op jit(solution)/shard_map/ppermute | solution.py:45
  310.1 14.4 %collective-permute-start.29 = (f32[5,16,1,8,128]{4,0,3,2,1:T(8,128)S(1)}, f32[5,16,1,8,128]{4,0,3,2,1:T(8,128)S(1)}, u32[]{:S(2)}, u32[]{:S(2)}) collective-permute-start(f32[5,16,1,8,128]{4,0,3,2,1:T(8,128)S(1)} %get-tuple-element.29), channel_id=1, source_target_pairs={{4,0},{8,4},{12,8},{16,12},{20,16},{24,20},{28,24},{5,1},{9,5},{13... | collective-permute-start | bytes 983048 | tf_op jit(solution)/shard_map/ppermute | solution.py:46
  324.6 15.5 %collective-permute-start.32 = (f32[5,16,6,1,128]{4,0,3,2,1:T(8,128)S(1)}, f32[5,16,6,1,128]{4,0,3,2,1:T(8,128)S(1)}, u32[]{:S(2)}, u32[]{:S(2)}) collective-permute-start(f32[5,16,6,1,128]{4,0,3,2,1:T(8,128)S(1)} %get-tuple-element.10), channel_id=1, source_target_pairs={{0,1},{1,2},{2,3},{4,5},{5,6},{6,7},{8,9},{9,10},{10,11},{12,13},{... | collective-permute-start | bytes 737288 | tf_op jit(solution)/shard_map/ppermute | solution.py:45
  349.2 11.6 %collective-permute-start.34 = (f32[5,16,1,8,128]{4,0,3,2,1:T(8,128)S(1)}, f32[5,16,1,8,128]{4,0,3,2,1:T(8,128)S(1)}, u32[]{:S(2)}, u32[]{:S(2)}) collective-permute-start(f32[5,16,1,8,128]{4,0,3,2,1:T(8,128)S(1)} %get-tuple-element.24), channel_id=1, source_target_pairs={{0,4},{4,8},{8,12},{12,16},{16,20},{20,24},{24,28},{1,5},{5,9},{9,... | collective-permute-start | bytes 983048 | tf_op jit(solution)/shard_map/ppermute | solution.py:45
  353.6 15.3 %collective-permute-start.33 = (f32[5,16,1,8,128]{4,0,3,2,1:T(8,128)S(1)}, f32[5,16,1,8,128]{4,0,3,2,1:T(8,128)S(1)}, u32[]{:S(2)}, u32[]{:S(2)}) collective-permute-start(f32[5,16,1,8,128]{4,0,3,2,1:T(8,128)S(1)} %get-tuple-element.25), channel_id=1, source_target_pairs={{4,0},{8,4},{12,8},{16,12},{20,16},{24,20},{28,24},{5,1},{9,5},{13... | collective-permute-start | bytes 983048 | tf_op jit(solution)/shard_map/ppermute | solution.py:46
  369.0 14.4 %collective-permute-start.36 = (f32[5,16,6,1,128]{4,0,3,2,1:T(8,128)S(1)}, f32[5,16,6,1,128]{4,0,3,2,1:T(8,128)S(1)}, u32[]{:S(2)}, u32[]{:S(2)}) collective-permute-start(f32[5,16,6,1,128]{4,0,3,2,1:T(8,128)S(1)} %get-tuple-element.8), channel_id=1, source_target_pairs={{0,1},{1,2},{2,3},{4,5},{5,6},{6,7},{8,9},{9,10},{10,11},{12,13},{... | collective-permute-start | bytes 737288 | tf_op jit(solution)/shard_map/ppermute | solution.py:45
  (35 other events, 221.2 us)
